TPU v7x, 32 devices: a whole 2x2x4 slice. The times are simulated.
32 devices in a mesh: dp: 16 (over z, y, x), section: 2 (over core).
Axes of the slice: x: 2, y: 2, z: 4, core: 2. Of those that a mesh axis runs over, the one named last changes fastest.
Arguments:
- section_inputs: bfloat16 [2, 2, 2048, 2048], P('section', None, 'dp'), may hold values from -6 to 6
- mix_weight: bfloat16 [2, 2048, 2048], P('section'), may hold values from -0.0625 to 0.0625
- norm_gain: float32 [2, 2048], P('section'), may hold values from 0.5 to 1.5
- out_cotangent: bfloat16 [2, 2048, 2048], P(None, 'dp'), may hold values from -6 to 6
- positions: int32 [2, 2048], P(None, 'dp'), may hold values from 0 to 1023
Outputs:
- grad_inputs: bfloat16 [2, 2, 2048, 2048], P('section', None, 'dp')
- grad_weight: float32 [2, 2048, 2048], P('section', 'dp')
- grad_gain: float32 [2, 2048], P('section', 'dp')
Inputs may be any that keep to these rules, and one draw needn't show every extreme that they name: `positions`: depth index of a token within its tile.
All inputs are finite; a program needn't handle non-finite values.
Results may differ from a plain program's by a relative error of at most 0.017.
Values may be sent and summed in bfloat16 or wider, within the bound.
A program may use at most 128 MiB of HBM per device.

v0:
```python
import functools
import math

import jax
import jax.numpy as jnp
from jax import lax
from jax.experimental import pallas as pl
from jax.experimental.pallas import tpu as pltpu
from jax.sharding import PartitionSpec as P

DEPTH = 1024
MESH = pl.DeviceIdType.MESH
F32 = jnp.float32
BF16 = jnp.bfloat16


def outer_sum(a, b):
    return lax.dot_general(a, b, (((0,), (0,)), ((), ())), preferred_element_type=F32)


ROOT = math.sqrt(2.0 / math.pi)
CUBE = 0.044715
CHUNKS = 2


def back_kernel(
    planes, sections, x_hbm, w_hbm, cot_hbm, gain_ref, factor_ref, out_ref, gain_out, grads_ref,
    x_ref, w_ref, g_ref, slope, act_ref, up_ref, q_ref, m_ref, proj,
    gath_a, gath_u, part, from_left, from_right, to_right, to_left, swap_out, swap_in,
    gain_own, gain_in, gain_mid, gain_sum, gain_z,
    in_sem, sec_send, sec_recv, u_send, u_recv, s_send, s_recv,
    xy_send, xy_recv, r_send, r_recv, l_send, l_recv, g_send, g_recv,
):
    me = lax.axis_index("dp")
    sec = lax.axis_index("section")
    last = sections - 1
    total = planes * 4
    x = lax.rem(me, 2)
    y = lax.rem(me // 2, 2)
    z = me // 4
    xn = me + 1 - 2 * x
    yn = me + 2 - 4 * y
    tokens, channels = x_ref.shape
    half = channels // 2
    rows = half // planes
    share = rows // 2
    micro, tok_mb = factor_ref.shape
    step_rows = 16
    width = min(256, channels)
    part_cols = half // CHUNKS

    load_x = pltpu.make_async_copy(x_hbm, x_ref, in_sem.at[0])
    load_w = pltpu.make_async_copy(w_hbm, w_ref, in_sem.at[1])
    load_g = pltpu.make_async_copy(cot_hbm, g_ref, in_sem.at[2])
    load_x.start()

    def copy(src, dst, send, recv, to):
        return pltpu.make_async_remote_copy(
            src_ref=src, dst_ref=dst, send_sem=send, recv_sem=recv,
            device_id={"dp": to}, device_id_type=MESH,
        )

    barrier = pltpu.get_barrier_semaphore()
    z_peers = [lax.rem(me + 4 * step, total) for step in range(1, planes)]
    for peer in [xn, yn] + z_peers:
        pl.semaphore_signal(barrier, inc=1, device_id={"dp": peer}, device_id_type=MESH)

    @pl.when(sec > 0)
    def _():
        pl.semaphore_signal(barrier, inc=1, device_id={"section": sec - 1}, device_id_type=MESH)

    @pl.when(sec < last)
    def _():
        pl.semaphore_signal(barrier, inc=1, device_id={"section": sec + 1}, device_id_type=MESH)

    @pl.when(sec == last)
    def _():
        load_g.start()

    load_w.start()

    for mb in range(micro):
        m_ref[mb * tok_mb:(mb + 1) * tok_mb, :] = jnp.transpose(
            jnp.broadcast_to(factor_ref[mb:mb + 1, :], (128, tok_mb))
        )
    proj[...] = jnp.zeros_like(proj)
    load_x.wait()

    @pl.loop(0, tokens // step_rows)
    def _(i):
        r = pl.ds(pl.multiple_of(i * step_rows, step_rows), step_rows)
        square = jnp.zeros((step_rows, rows), F32)
        for c in range(channels // rows):
            xc = x_ref[r, c * rows:(c + 1) * rows].astype(F32)
            square = square + xc * xc
        q = lax.rsqrt(jnp.sum(square, axis=-1, keepdims=True) / channels + 1e-06)
        q_ref[r, :] = jnp.broadcast_to(q, (step_rows, 128))
        for c in range(channels // rows):
            cols = slice(c * rows, (c + 1) * rows)
            n = x_ref[r, cols].astype(F32) * q * gain_ref[:, cols]
            n2 = n * n
            th = jnp.tanh(ROOT * (n + CUBE * (n2 * n)))
            cdf = 0.5 * (1.0 + th)
            act_ref[c % 2, r, (c // 2) * rows:(c // 2 + 1) * rows] = (n * cdf).astype(BF16)
            slope[r, cols] = cdf + (0.5 * ROOT) * n * (1.0 - th * th) * (1.0 + (3.0 * CUBE) * n2)

    beside = jnp.minimum(sec, 1) + jnp.minimum(last - sec, 1)
    pl.semaphore_wait(barrier, 1 + planes + beside)

    act_y = copy(act_ref.at[1 - y], gath_a.at[1], xy_send.at[0], xy_recv.at[0], yn)
    act_x = copy(act_ref.at[y], gath_a.at[0], xy_send.at[1], xy_recv.at[1], xn)
    up_x = [
        copy(up_ref.at[(1 - x) * CHUNKS + k], gath_u.at[k], u_send.at[k], u_recv.at[k], xn)
        for k in range(CHUNKS)
    ]
    up_y = [
        copy(
            up_ref.at[x * CHUNKS + k], gath_u.at[CHUNKS + k],
            u_send.at[CHUNKS + k], u_recv.at[CHUNKS + k], yn,
        )
        for k in range(CHUNKS)
    ]
    up_d = [
        copy(
            gath_u.at[k], gath_u.at[2 * CHUNKS + k],
            u_send.at[2 * CHUNKS + k], u_recv.at[2 * CHUNKS + k], yn,
        )
        for k in range(CHUNKS)
    ]
    act_d = copy(gath_a.at[1], gath_a.at[2], xy_send.at[4], xy_recv.at[4], xn)
    gain_x = copy(gain_own, gain_in.at[0], g_send.at[0], g_recv.at[0], xn)
    gain_y = copy(gain_mid, gain_in.at[1], g_send.at[1], g_recv.at[1], yn)
    def relay(mb):
        span = pl.ds(mb * tok_mb, tok_mb)
        return pltpu.make_async_remote_copy(
            src_ref=grads_ref.at[span, :], dst_ref=g_ref.at[span, :],
            send_sem=sec_send.at[mb], recv_sem=sec_recv.at[mb],
            device_id={"section": jnp.maximum(sec - 1, 0)}, device_id_type=MESH,
        )

    @pl.when(sec < last)
    def _():
        relay(0).wait_recv()

    act_y.start()
    act_x.start()

    @pl.when(sec == last)
    def _():
        load_g.wait()

    for mb in range(micro):
        if mb > 0:
            @pl.when(sec < last)
            def _():
                relay(mb).wait_recv()

        @pl.loop(mb * (tok_mb // step_rows), (mb + 1) * (tok_mb // step_rows))
        def _(i):
            r = pl.ds(pl.multiple_of(i * step_rows, step_rows), step_rows)
            m = m_ref[r, :1]
            for h in range(2 * CHUNKS):
                g = g_ref[r, h * part_cols:(h + 1) * part_cols].astype(F32)
                up_ref[h, r, :] = (m * g).astype(BF16)

    up_x[0].start()
    up_y[0].start()
    load_w.wait()

    @pl.loop(0, channels // width)
    def _(c):
        cols = pl.ds(pl.multiple_of(c * width, width), width)
        last_dims = (((1,), (1,)), ((), ()))
        back = jnp.zeros((tokens, width), F32)
        for h in range(2 * CHUNKS):
            back = back + lax.dot_general(
                up_ref[h], w_ref[cols, h * part_cols:(h + 1) * part_cols], last_dims,
                preferred_element_type=F32,
            )
        grad_norm = back * slope[:, cols]
        xc = x_ref[:, cols].astype(F32)
        scaled = grad_norm * gain_ref[:, cols]
        slope[:, cols] = scaled
        along = scaled * xc
        lanes = proj[...]
        for k in range(width // 128):
            lanes = lanes + along[:, k * 128:(k + 1) * 128]
        proj[...] = lanes
        gain_own[:, cols] = jnp.sum(grad_norm * xc * q_ref[:, :1], axis=0, keepdims=True)

    for mb in range(micro):
        @pl.loop(mb * (tok_mb // step_rows), (mb + 1) * (tok_mb // step_rows))
        def _(i):
            r = pl.ds(pl.multiple_of(i * step_rows, step_rows), step_rows)
            q = q_ref[r, :1]
            pull = (q * q * q) * (jnp.sum(proj[r, :], axis=-1, keepdims=True) / channels)
            for c in range(channels // width):
                cols = slice(c * width, (c + 1) * width)
                delta = q * slope[r, cols] - x_ref[r, cols].astype(F32) * pull
                grads_ref[r, cols] = (g_ref[r, cols].astype(F32) + delta).astype(BF16)

        @pl.when(sec > 0)
        def _():
            relay(mb).start()

    act_y.wait_recv()
    act_d.start()
    up_x[0].wait_recv()
    up_d[0].start()
    gain_x.start()
    for k in range(1, CHUNKS):
        up_x[k].start()
        up_y[k].start()

    for k in range(CHUNKS):
        @pl.loop(0, planes)
        def _(b):
            cols = pl.ds(pl.multiple_of(b * rows, 128), rows)
            part[k * planes + b] = outer_sum(act_ref[y, :, cols], up_ref[x * CHUNKS + k])

    def add_source(slot, k):
        @pl.loop(0, planes)
        def _(b):
            cols = pl.ds(pl.multiple_of(b * rows, 128), rows)
            part[k * planes + b] += outer_sum(gath_a[slot, :, cols], gath_u[slot * CHUNKS + k])

    z_next = lax.rem(me + 4, total)
    z_prev = lax.rem(me + total - 4, total)

    def right(at):
        return copy(to_right.at[at], from_left.at[at], r_send.at[at], r_recv.at[at], z_next)

    def left(at):
        return copy(to_left.at[at], from_right.at[at], l_send.at[at], l_recv.at[at], z_prev)

    def z_step(t, k):
        @pl.when(t >= z)
        def _():
            at = k * planes + planes - 1 - t + z

            @pl.when(z > 0)
            def _():
                right(at).wait_recv()
                to_right[at] = (part[at] + from_left[at].astype(F32)).astype(BF16)

            @pl.when(z == 0)
            def _():
                to_right[at] = part[at].astype(BF16)

            right(at).start()

        @pl.when(t >= planes - 1 - z)
        def _():
            at = k * planes + t - (planes - 1 - z)

            @pl.when(z < planes - 1)
            def _():
                left(at).wait_recv()
                to_left[at] = (part[at] + from_right[at].astype(F32)).astype(BF16)

            @pl.when(z == planes - 1)
            def _():
                to_left[at] = part[at].astype(BF16)

            left(at).start()

    act_x.wait_recv()
    for k in range(CHUNKS):
        if k == 0:
            add_source(0, 0)
        up_y[k].wait_recv()
        add_source(1, k)
        if k == 0:
            act_d.wait_recv()
        up_d[k].wait_recv()
        add_source(2, k)
        z_step(0, k)
        if k + 1 < CHUNKS:
            up_x[k + 1].wait_recv()
            up_d[k + 1].start()
        for t in range(1, planes - 1):
            z_step(t, k)
        if k + 1 < CHUNKS:
            add_source(0, k + 1)

    gain_x.wait_recv()
    gain_mid[...] = gain_own[...] + gain_in[0]
    gain_y.start()
    other = pl.ds(pl.multiple_of((1 - x) * share, 64), share)
    own = pl.ds(pl.multiple_of(x * share, 64), share)
    swaps = [
        copy(swap_out.at[k], swap_in.at[k], s_send.at[k], s_recv.at[k], xn)
        for k in range(CHUNKS)
    ]

    def finish(k):
        at = k * planes + z

        @pl.when(z > 0)
        def _():
            right(at).wait_recv()
            part[at] += from_left[at].astype(F32)

        @pl.when(z < planes - 1)
        def _():
            left(at).wait_recv()
            part[at] += from_right[at].astype(F32)

        swap_out[k] = part[at, other, :].astype(BF16)
        swaps[k].start()
        for side in range(2):
            @pl.when(x == side)
            def _():
                lo = side * half + k * part_cols
                out_ref[:, lo:lo + part_cols] = part[at, own, :]

    for k in range(CHUNKS - 1):
        finish(k)
    gain_y.wait_recv()
    gain_sum[...] = gain_mid[...] + gain_in[1]
    gain_zs = [
        copy(gain_sum, gain_z.at[step], g_send.at[2 + step], g_recv.at[2 + step], z_peers[step])
        for step in range(planes - 1)
    ]
    for tiny in gain_zs:
        tiny.start()

    finish(CHUNKS - 1)
    for tiny in gain_zs:
        tiny.wait_recv()
    total_gain = gain_sum[...]
    for step in range(planes - 1):
        total_gain = total_gain + gain_z[step]
    gain_out[...] = total_gain

    for k in range(CHUNKS):
        swaps[k].wait_recv()
        for side in range(2):
            @pl.when(x == side)
            def _():
                lo = (1 - side) * half + k * part_cols
                out_ref[:, lo:lo + part_cols] = swap_in[k].astype(F32)

    for sent in [act_x, act_y, act_d, gain_x, gain_y] + up_x + up_y + up_d + swaps + gain_zs:
        sent.wait_send()
    for k in range(CHUNKS):
        for t in range(planes - 1):
            @pl.when(t >= z)
            def _():
                right(k * planes + planes - 1 - t + z).wait_send()

            @pl.when(t >= planes - 1 - z)
            def _():
                left(k * planes + t - (planes - 1 - z)).wait_send()

    @pl.when(sec > 0)
    def _():
        for mb in range(micro):
            relay(mb).wait_send()


def body(section_inputs, mix_weight, norm_gain, out_cotangent, positions):
    sections = lax.axis_size("section")
    micro, tok_mb, channels = section_inputs.shape[1:]
    tokens = micro * tok_mb
    count = lax.axis_size("dp")
    planes = count // 4
    share = channels // count
    half = channels // 2
    rows = half // planes
    factor = 1.0 + 0.5 * jnp.sin(2.0 * math.pi * positions.astype(F32) / DEPTH)
    vmem = pl.BlockSpec(memory_space=pltpu.VMEM)
    hbm = pl.BlockSpec(memory_space=pltpu.HBM)
    part_cols = half // CHUNKS
    hops = CHUNKS * planes
    block = (hops, rows, part_cols)
    line = (1, channels)
    sems = pltpu.SemaphoreType.DMA
    weight_grad, gain_all, grads = pl.pallas_call(
        functools.partial(back_kernel, planes, sections),
        out_shape=(
            jax.ShapeDtypeStruct((share, channels), F32),
            jax.ShapeDtypeStruct(line, F32),
            jax.ShapeDtypeStruct((tokens, channels), BF16),
        ),
        in_specs=[hbm, hbm, hbm, vmem, vmem],
        out_specs=(vmem, vmem, vmem),
        scratch_shapes=[
            pltpu.VMEM((tokens, channels), BF16),
            pltpu.VMEM((channels, channels), BF16),
            pltpu.VMEM((tokens, channels), BF16),
            pltpu.VMEM((tokens, channels), F32),
            pltpu.VMEM((2, tokens, half), BF16),
            pltpu.VMEM((2 * CHUNKS, tokens, part_cols), BF16),
            pltpu.VMEM((tokens, 128), F32),
            pltpu.VMEM((tokens, 128), F32),
            pltpu.VMEM((tokens, 128), F32),
            pltpu.VMEM((3, tokens, half), BF16),
            pltpu.VMEM((3 * CHUNKS, tokens, part_cols), BF16),
            pltpu.VMEM(block, F32),
            pltpu.VMEM(block, BF16),
            pltpu.VMEM(block, BF16),
            pltpu.VMEM(block, BF16),
            pltpu.VMEM(block, BF16),
            pltpu.VMEM((CHUNKS, share, part_cols), BF16),
            pltpu.VMEM((CHUNKS, share, part_cols), BF16),
            pltpu.VMEM(line, F32),
            pltpu.VMEM((2,) + line, F32),
            pltpu.VMEM(line, F32),
            pltpu.VMEM(line, F32),
            pltpu.VMEM((planes - 1,) + line, F32),
            sems((3,)), sems((micro,)), sems((micro,)),
            sems((3 * CHUNKS,)), sems((3 * CHUNKS,)), sems((CHUNKS,)), sems((CHUNKS,)),
            sems((5,)), sems((5,)), sems((hops,)), sems((hops,)),
            sems((hops,)), sems((hops,)), sems((planes + 1,)), sems((planes + 1,)),
        ],
        compiler_params=pltpu.CompilerParams(
            collective_id=0, has_side_effects=True, vmem_limit_bytes=50 << 20
        ),
    )(
        section_inputs.reshape(tokens, channels),
        mix_weight[0],
        out_cotangent.reshape(tokens, channels),
        norm_gain,
        factor,
    )
    gain_share = lax.dynamic_slice_in_dim(gain_all[0], lax.axis_index("dp") * share, share, 0)
    return (grads.reshape(1, micro, tok_mb, channels), weight_grad[None], gain_share[None])


def solution(mesh):
    return jax.shard_map(
        body,
        mesh=mesh,
        in_specs=(
            P("section", None, "dp", None),
            P("section", None, None),
            P("section", None),
            P(None, "dp", None),
            P(None, "dp"),
        ),
        out_specs=(P("section", None, "dp", None), P("section", "dp", None), P("section", "dp")),
        check_vma=False,
    )
```

profile of v0, /device:TPU:0, one launch (start us, length us, event | category | flops | bytes accessed | tf_op | source)
XLA Modules:
  0.0 84.9 jit_solution(10039249831344254470)
XLA Ops:
  0.6 0.7 multiply_add_fusion.factor_ref
  1.4 0.0 copy-start
  1.4 1.2 %copy-done = bf16[1,2,128,2048]{3,2,1,0:T(8,128)(2,1)S(1)} copy-done((bf16[1,2,128,2048]{3,2,1,0:T(8,128)(2,1)S(1)}, bf16[1,2,128,2048]{3,2,1,0:T(8,128)(2,1)}, u32[]{:S(2)}) %copy-start) | copy-done | bytes 1048600
  2.6 0.0 copy-start.1
  2.6 0.7 copy-done.1
  3.3 79.1 %shard_map.76 = (f32[128,2048]{1,0:T(8,128)S(1)}, f32[1,2048]{1,0:T(1,128)S(1)}, bf16[256,2048]{1,0:T(8,128)(2,1)S(1)}) custom-call(bf16[256,2048]{1,0:T(8,128)(2,1)S(1)} %bitcast.5, bf16[2048,2048]{1,0:T(8,128)(2,1)} %bitcast.8, bf16[256,2048]{1,0:T(8,128)(2,1)} %bitcast.9, f32[1,2048]{1,0:T(1,128)S(1)} %copy-done.1, f32[2,128]{1,0:T(2,128)S(1)} %multiply_add_fusion.factor_ref), custom_call_target="tpu_custom_call" | custom-call | tf_op jit(solution)/shard_map/pallas_call | solution.py:379
  82.4 0.5 constant_dynamic-slice_fusion
  83.0 1.0 %copy.10 = bf16[1,2,128,2048]{3,2,1,0:T(8,128)(2,1)} copy(bf16[1,2,128,2048]{3,2,1,0:T(8,128)(2,1)S(1)} %bitcast.7) | data formatting | bytes 2097152
  83.9 1.0 %copy.11 = f32[1,128,2048]{2,1,0:T(8,128)} copy(f32[1,128,2048]{2,1,0:T(8,128)S(1)} %bitcast.6) | data formatting | bytes 2097152
Async XLA Ops:
  1.4 1.2 %copy-start = (bf16[1,2,128,2048]{3,2,1,0:T(8,128)(2,1)S(1)}, bf16[1,2,128,2048]{3,2,1,0:T(8,128)(2,1)}, u32[]{:S(2)}) copy-start(bf16[1,2,128,2048]{3,2,1,0:T(8,128)(2,1)} %param.5) | copy-start | bytes 3145732
  2.6 0.7 copy-start.1
where the time goes:
time: 85.1 us; the launch traced here: 84.9 us
  Pallas kernels  79.1 us (93%)
  local copies, waits for them, and re-layouts  4.38 us (5%)
    pallas_call x1, Pallas kernels, body(): pl.pallas_call(functools.partial(back_kernel, planes, sections), out_shap...  79.1 us
    unnamed x6, local copies, waits for them, and re-layouts  3.86 us

commit v1 on v0

v1 whole, which is shorter than its diff:
```python
import functools
import math

import jax
import jax.numpy as jnp
from jax import lax
from jax.experimental import pallas as pl
from jax.experimental.pallas import tpu as pltpu
from jax.sharding import PartitionSpec as P

DEPTH = 1024
MESH = pl.DeviceIdType.MESH
F32 = jnp.float32
BF16 = jnp.bfloat16
ROOT = math.sqrt(2.0 / math.pi)
CUBE = 0.044715
CHUNKS = 4


def contract(a, b, dims):
    return lax.dot_general(a, b, (dims, ((), ())), preferred_element_type=F32)


def block_order(planes, chunks):
    pairs = planes // 2
    first = [(i, k) for i in range(pairs) for k in range(2)]
    return first + [(i, k) for k in range(2, chunks) for i in range(pairs)]


def back_kernel(
    planes, sections, x_hbm, w_hbm, cot_hbm, gain_hbm, pos_hbm, out_ref, gain_out, grads_ref,
    x_ref, w_ref, g_ref, gain_ref, pos_ref, slope, tmp, eye_ref, act_ref, up_ref, q_ref, m_ref,
    proj, gath_a, gath_u, part, from_left, from_right, to_right, to_left, swap_out, swap_in,
    gain_own, gain_in, gain_mid, gain_sum, gain_z,
    in_sem, sec_send, sec_recv, u_send, u_recv, a_send, a_recv, s_send, s_recv,
    r_send, r_recv, l_send, l_recv, g_send, g_recv,
):
    me = lax.axis_index("dp")
    sec = lax.axis_index("section")
    last = sections - 1
    total = planes * 4
    x = lax.rem(me, 2)
    y = lax.rem(me // 2, 2)
    z = me // 4
    xn = me + 1 - 2 * x
    yn = me + 2 - 4 * y
    tokens, channels = x_ref.shape
    half = channels // 2
    rows = half // planes
    share = rows // 2
    micro, tok_mb = pos_ref.shape
    step_rows = 16
    width = min(256, channels)
    part_cols = half // CHUNKS
    pairs = planes // 2

    load_x = pltpu.make_async_copy(x_hbm, x_ref, in_sem.at[0])
    load_w = pltpu.make_async_copy(w_hbm, w_ref, in_sem.at[1])
    load_g = pltpu.make_async_copy(cot_hbm, g_ref, in_sem.at[2])
    load_gain = pltpu.make_async_copy(gain_hbm, gain_ref, in_sem.at[3])
    load_pos = pltpu.make_async_copy(pos_hbm, pos_ref, in_sem.at[4])
    load_pos.start()

    @pl.when(sec == last)
    def _():
        load_g.start()

    load_x.start()
    load_gain.start()
    load_w.start()

    def copy(src, dst, send, recv, to):
        return pltpu.make_async_remote_copy(
            src_ref=src, dst_ref=dst, send_sem=send, recv_sem=recv,
            device_id={"dp": to}, device_id_type=MESH,
        )

    barrier = pltpu.get_barrier_semaphore()
    z_peers = [lax.rem(me + 4 * step, total) for step in range(1, planes)]
    for peer in [xn, yn] + z_peers:
        pl.semaphore_signal(barrier, inc=1, device_id={"dp": peer}, device_id_type=MESH)

    @pl.when(sec > 0)
    def _():
        pl.semaphore_signal(barrier, inc=1, device_id={"section": sec - 1}, device_id_type=MESH)

    @pl.when(sec < last)
    def _():
        pl.semaphore_signal(barrier, inc=1, device_id={"section": sec + 1}, device_id_type=MESH)

    proj[...] = jnp.zeros_like(proj)
    at_row = lax.broadcasted_iota(jnp.int32, (rows, rows), 0)
    at_col = lax.broadcasted_iota(jnp.int32, (rows, rows), 1)
    eye_ref[...] = jnp.where(at_row == at_col, 1.0, 0.0).astype(BF16)
    with jax.named_scope("w_pos"):
        load_pos.wait()
    factor = 1.0 + 0.5 * jnp.sin(2.0 * math.pi * pos_ref[...].astype(F32) / DEPTH)
    for mb in range(micro):
        m_ref[mb * tok_mb:(mb + 1) * tok_mb, :] = jnp.transpose(
            jnp.broadcast_to(factor[mb:mb + 1, :], (128, tok_mb))
        )

    ux = [
        copy(up_ref.at[(1 - x) * CHUNKS + k], gath_u.at[k], u_send.at[k], u_recv.at[k], xn)
        for k in range(CHUNKS)
    ]
    uy = [
        copy(
            up_ref.at[x * CHUNKS + k], gath_u.at[CHUNKS + k],
            u_send.at[CHUNKS + k], u_recv.at[CHUNKS + k], yn,
        )
        for k in range(CHUNKS)
    ]
    ud = [
        copy(
            gath_u.at[k], gath_u.at[2 * CHUNKS + k],
            u_send.at[2 * CHUNKS + k], u_recv.at[2 * CHUNKS + k], yn,
        )
        for k in range(CHUNKS)
    ]
    spans = [pl.ds(b * rows, rows) for b in range(planes)]
    ax = [
        copy(act_ref.at[y, spans[b]], gath_a.at[0, spans[b]], a_send.at[b], a_recv.at[b], xn)
        for b in range(planes)
    ]
    ay = [
        copy(
            act_ref.at[1 - y, spans[b]], gath_a.at[1, spans[b]],
            a_send.at[planes + b], a_recv.at[planes + b], yn,
        )
        for b in range(planes)
    ]
    ad = [
        copy(
            gath_a.at[1, spans[b]], gath_a.at[2, spans[b]],
            a_send.at[2 * planes + b], a_recv.at[2 * planes + b], xn,
        )
        for b in range(planes)
    ]
    gain_x = copy(gain_own, gain_in.at[0], g_send.at[0], g_recv.at[0], xn)
    gain_y = copy(gain_mid, gain_in.at[1], g_send.at[1], g_recv.at[1], yn)

    def relay(mb):
        span = pl.ds(mb * tok_mb, tok_mb)
        return pltpu.make_async_remote_copy(
            src_ref=grads_ref.at[span, :], dst_ref=g_ref.at[span, :],
            send_sem=sec_send.at[mb], recv_sem=sec_recv.at[mb],
            device_id={"section": jnp.maximum(sec - 1, 0)}, device_id_type=MESH,
        )

    arrived = set()

    def arrive(name, sent):
        if name not in arrived:
            arrived.add(name)
            with jax.named_scope("w_" + name):
                sent.wait_recv()

    def forward_u(k):
        arrive("ux%d" % k, ux[k])
        ud[k].start()

    def forward_a(b):
        arrive("ay%d" % b, ay[b])
        ad[b].start()

    def upstream(mb):
        @pl.loop(mb * (tok_mb // step_rows), (mb + 1) * (tok_mb // step_rows))
        def _(i):
            r = pl.ds(pl.multiple_of(i * step_rows, step_rows), step_rows)
            m = m_ref[r, :]
            for c in range(channels // 128):
                at = c * 128
                g = g_ref[r, at:at + 128].astype(F32)
                low = at % part_cols
                up_ref[at // part_cols, r, low:low + 128] = (m * g).astype(BF16)

    @pl.when(sec == last)
    def _():
        with jax.named_scope("w_g"):
            load_g.wait()
        for mb in range(micro):
            upstream(mb)

    beside = jnp.minimum(sec, 1) + jnp.minimum(last - sec, 1)
    with jax.named_scope("barrier"):
        pl.semaphore_wait(barrier, 1 + planes + beside)

    @pl.when(sec == last)
    def _():
        ux[0].start()
        uy[0].start()

    with jax.named_scope("w_x"):
        load_x.wait()
        load_gain.wait()

    @pl.loop(0, tokens // step_rows)
    def _(i):
        r = pl.ds(pl.multiple_of(i * step_rows, step_rows), step_rows)
        square = jnp.zeros((step_rows, rows), F32)
        for c in range(channels // rows):
            xc = x_ref[r, c * rows:(c + 1) * rows].astype(F32)
            square = square + xc * xc
        q = lax.rsqrt(jnp.sum(square, axis=-1, keepdims=True) / channels + 1e-06)
        q_ref[r, :] = jnp.broadcast_to(q, (step_rows, 128))

    tall = 32

    def activate(b):
        @pl.loop(0, tokens // tall)
        def _(i):
            r = pl.ds(pl.multiple_of(i * tall, tall), tall)
            q = q_ref[r, :]
            for c in range(2 * rows // 128):
                at = 2 * b * rows + c * 128
                cols = slice(at, at + 128)
                low = c * 128 % rows
                n = x_ref[r, cols].astype(F32) * q * gain_ref[:, cols]
                n2 = n * n
                th = jnp.tanh(ROOT * (n + CUBE * (n2 * n)))
                cdf = 0.5 * (1.0 + th)
                tmp[c * 128 // rows, r, low:low + 128] = (n * cdf).astype(BF16)
                slope[r, cols] = cdf + (0.5 * ROOT) * n * (1.0 - th * th) * (1.0 + (3.0 * CUBE) * n2)

        for side in range(2):
            act_ref[side, spans[b], :] = contract(eye_ref[...], tmp[side], ((1,), (1,))).astype(BF16)

    order = []
    for i in range(pairs):
        order += [i, planes - 1 - i]
    for n, b in enumerate(order):
        activate(b)
        if n < 2:
            @pl.when(sec == last)
            def _():
                ay[b].start()
                ax[b].start()

    @pl.when(sec < last)
    def _():
        for mb in range(micro):
            with jax.named_scope("w_relay%d" % mb):
                relay(mb).wait_recv()
            upstream(mb)
        ux[0].start()
        uy[0].start()
        for b in order[:2]:
            ay[b].start()
            ax[b].start()

    forward_u(0)
    with jax.named_scope("w_w"):
        load_w.wait()

    def back_columns(start, stop):
        @pl.loop(start, stop)
        def _(c):
            cols = pl.ds(pl.multiple_of(c * width, width), width)
            back = jnp.zeros((tokens, width), F32)
            for h in range(2 * CHUNKS):
                back = back + contract(
                    up_ref[h], w_ref[cols, h * part_cols:(h + 1) * part_cols], ((1,), (1,))
                )
            lanes = proj[...]
            q = q_ref[...]
            for k in range(width // 128):
                piece = pl.ds(pl.multiple_of(c * width + k * 128, 128), 128)
                grad_norm = back[:, k * 128:(k + 1) * 128] * slope[:, piece]
                xc = x_ref[:, piece].astype(F32)
                scaled = grad_norm * gain_ref[:, piece]
                slope[:, piece] = scaled
                lanes = lanes + scaled * xc
                gain_own[:, piece] = jnp.sum(grad_norm * xc * q, axis=0, keepdims=True)
            proj[...] = lanes

    steps = channels // width
    back_columns(0, steps // 4)
    forward_a(order[0])
    back_columns(steps // 4, steps // 2)
    forward_a(order[1])
    ux[1].start()
    for b in order[2:]:
        ay[b].start()
        ax[b].start()
    uy[1].start()
    back_columns(steps // 2, steps)
    gain_x.start()

    for mb in range(micro):
        @pl.loop(mb * (tok_mb // step_rows), (mb + 1) * (tok_mb // step_rows))
        def _(i):
            r = pl.ds(pl.multiple_of(i * step_rows, step_rows), step_rows)
            q = q_ref[r, :]
            along = jnp.sum(proj[r, :], axis=-1, keepdims=True) / channels
            pull = (q * q * q) * jnp.broadcast_to(along, (step_rows, 128))
            for c in range(channels // 128):
                cols = slice(c * 128, (c + 1) * 128)
                delta = q * slope[r, cols] - x_ref[r, cols].astype(F32) * pull
                grads_ref[r, cols] = (g_ref[r, cols].astype(F32) + delta).astype(BF16)

        @pl.when(sec > 0)
        def _():
            relay(mb).start()

    z_next = lax.rem(me + 4, total)
    z_prev = lax.rem(me + total - 4, total)

    def right(at):
        return copy(to_right.at[at], from_left.at[at], r_send.at[at], r_recv.at[at], z_next)

    def left(at):
        return copy(to_left.at[at], from_right.at[at], l_send.at[at], l_recv.at[at], z_prev)

    def products(i, k):
        for b in (i, planes - 1 - i):
            arrive("ax%d" % b, ax[b])
            arrive("ad%d" % b, ad[b])
        arrive("uy%d" % k, uy[k])
        arrive("ud%d" % k, ud[k])

        @pl.loop(0, 2)
        def _(n):
            b = i + n * (planes - 1 - 2 * i)
            span = pl.ds(pl.multiple_of(b * rows, rows), rows)
            inner = ((1,), (0,))
            term = contract(act_ref[y, span, :], up_ref[x * CHUNKS + k], inner)
            for slot in range(3):
                term = term + contract(
                    gath_a[slot, span, :], gath_u[slot * CHUNKS + k], inner
                )
            part[k * planes + b] = term

    def stage(h, i, k):
        near = planes - 1 - h

        @pl.when(z == h)
        def _():
            for d in (planes - 1 - i, i):
                if d > h:
                    at = k * planes + d
                    if h > 0:
                        with jax.named_scope("w_r%d_%d" % (d, k)):
                            right(at).wait_recv()
                        to_right[at] = (part[at] + from_left[at].astype(F32)).astype(BF16)
                    else:
                        to_right[at] = part[at].astype(BF16)
                    right(at).start()

        @pl.when(z == near)
        def _():
            for d in (i, planes - 1 - i):
                if d < near:
                    at = k * planes + d
                    if h > 0:
                        with jax.named_scope("w_l%d_%d" % (d, k)):
                            left(at).wait_recv()
                        to_left[at] = (part[at] + from_right[at].astype(F32)).astype(BF16)
                    else:
                        to_left[at] = part[at].astype(BF16)
                    left(at).start()

    other = pl.ds(pl.multiple_of((1 - x) * share, 64), share)
    own = pl.ds(pl.multiple_of(x * share, 64), share)
    swaps = [
        copy(swap_out.at[k], swap_in.at[k], s_send.at[k], s_recv.at[k], xn)
        for k in range(CHUNKS)
    ]

    def finish(k):
        at = k * planes + z

        @pl.when(z > 0)
        def _():
            with jax.named_scope("w_fr%d" % k):
                right(at).wait_recv()
            part[at] += from_left[at].astype(F32)

        @pl.when(z < planes - 1)
        def _():
            with jax.named_scope("w_fl%d" % k):
                left(at).wait_recv()
            part[at] += from_right[at].astype(F32)

        swap_out[k] = part[at, other, :].astype(BF16)
        swaps[k].start()
        for side in range(2):
            @pl.when(x == side)
            def _():
                lo = side * half + k * part_cols
                out_ref[:, lo:lo + part_cols] = part[at, own, :]

    def settle(k):
        with jax.named_scope("w_swap%d" % k):
            swaps[k].wait_recv()
        for side in range(2):
            @pl.when(x == side)
            def _():
                lo = (1 - side) * half + k * part_cols
                out_ref[:, lo:lo + part_cols] = swap_in[k].astype(F32)

    gain_zs = [
        copy(gain_sum, gain_z.at[step], g_send.at[2 + step], g_recv.at[2 + step], z_peers[step])
        for step in range(planes - 1)
    ]
    reach = {}

    def begin(i, k):
        products(i, k)
        reach[i, k] = 1
        stage(0, i, k)

    def advance(i, k):
        if reach[i, k] <= planes - 2 - i:
            stage(reach[i, k], i, k)
            reach[i, k] += 1

    begin(0, 0)
    for b in order[2:]:
        forward_a(b)
    for k in range(2, CHUNKS):
        ux[k].start()
        uy[k].start()
    forward_u(1)
    advance(0, 0)
    begin(0, 1)
    advance(0, 0)
    for i in range(1, pairs):
        begin(i, 0)
        begin(i, 1)
    advance(0, 1)
    forward_u(2)
    arrive("gain_x", gain_x)
    gain_mid[...] = gain_own[...] + gain_in[0]
    gain_y.start()
    for i in range(1, pairs):
        advance(i, 0)
    advance(0, 1)
    for i in range(1, pairs):
        advance(i, 1)
    for k in range(2, CHUNKS):
        if k + 1 < CHUNKS:
            forward_u(k + 1)
        for i in range(pairs):
            begin(i, k)
        if k + 1 < CHUNKS:
            for i in range(pairs):
                advance(i, k)
        if k == 2:
            arrive("gain_y", gain_y)
            gain_sum[...] = gain_mid[...] + gain_in[1]
            for tiny in gain_zs:
                tiny.start()
    finish(0)
    done = 1
    while any(reach[i, k] <= planes - 2 - i for i, k in reach):
        for i, k in block_order(planes, CHUNKS):
            advance(i, k)
        if done < CHUNKS - 2:
            finish(done)
            settle(done - 1)
            done += 1
    for k in range(done, CHUNKS):
        finish(k)
        settle(k - 1)
    with jax.named_scope("w_gain"):
        for tiny in gain_zs:
            tiny.wait_recv()
    total_gain = gain_sum[...]
    for step in range(planes - 1):
        total_gain = total_gain + gain_z[step]
    gain_z[0] = total_gain
    for r in range(total):
        @pl.when(me == r)
        def _():
            gain_out[...] = gain_z[0, :, r * (channels // total):(r + 1) * (channels // total)]
    settle(CHUNKS - 1)

    for sent in [gain_x, gain_y] + ux + uy + ud + ax + ay + ad + swaps + gain_zs:
        sent.wait_send()
    for k in range(CHUNKS):
        for d in range(planes):
            @pl.when(d > z)
            def _():
                right(k * planes + d).wait_send()

            @pl.when(d < z)
            def _():
                left(k * planes + d).wait_send()

    @pl.when(sec > 0)
    def _():
        for mb in range(micro):
            relay(mb).wait_send()


def store_kernel(*refs):
    count = (len(refs) - 1) // 2
    sems = refs[-1]
    copies = [
        pltpu.make_async_copy(refs[n], refs[count + n], sems.at[n]) for n in range(count)
    ]
    for one in copies:
        one.start()
    for one in copies:
        one.wait()


def body(section_inputs, mix_weight, norm_gain, out_cotangent, positions):
    sections = lax.axis_size("section")
    micro, tok_mb, channels = section_inputs.shape[1:]
    tokens = micro * tok_mb
    count = lax.axis_size("dp")
    planes = count // 4
    share = channels // count
    half = channels // 2
    rows = half // planes
    vmem = pl.BlockSpec(memory_space=pltpu.VMEM)
    hbm = pl.BlockSpec(memory_space=pltpu.HBM)
    part_cols = half // CHUNKS
    hops = CHUNKS * planes
    block = (hops, rows, part_cols)
    line = (1, channels)
    sems = pltpu.SemaphoreType.DMA
    results = pl.pallas_call(
        functools.partial(back_kernel, planes, sections),
        out_shape=(
            jax.ShapeDtypeStruct((share, channels), F32),
            jax.ShapeDtypeStruct((1, share), F32),
            jax.ShapeDtypeStruct((tokens, channels), BF16),
        ),
        in_specs=[hbm] * 5,
        out_specs=(vmem, vmem, vmem),
        scratch_shapes=[
            pltpu.VMEM((tokens, channels), BF16),
            pltpu.VMEM((channels, channels), BF16),
            pltpu.VMEM((tokens, channels), BF16),
            pltpu.VMEM(line, F32),
            pltpu.VMEM((micro, tok_mb), jnp.int32),
            pltpu.VMEM((tokens, channels), F32),
            pltpu.VMEM((2, tokens, rows), BF16),
            pltpu.VMEM((rows, rows), BF16),
            pltpu.VMEM((2, half, tokens), BF16),
            pltpu.VMEM((2 * CHUNKS, tokens, part_cols), BF16),
            pltpu.VMEM((tokens, 128), F32),
            pltpu.VMEM((tokens, 128), F32),
            pltpu.VMEM((tokens, 128), F32),
            pltpu.VMEM((3, half, tokens), BF16),
            pltpu.VMEM((3 * CHUNKS, tokens, part_cols), BF16),
            pltpu.VMEM(block, F32),
            pltpu.VMEM(block, BF16),
            pltpu.VMEM(block, BF16),
            pltpu.VMEM(block, BF16),
            pltpu.VMEM(block, BF16),
            pltpu.VMEM((CHUNKS, share, part_cols), BF16),
            pltpu.VMEM((CHUNKS, share, part_cols), BF16),
            pltpu.VMEM(line, F32),
            pltpu.VMEM((2,) + line, F32),
            pltpu.VMEM(line, F32),
            pltpu.VMEM(line, F32),
            pltpu.VMEM((planes - 1,) + line, F32),
            sems((5,)), sems((micro,)), sems((micro,)),
            sems((3 * CHUNKS,)), sems((3 * CHUNKS,)), sems((3 * planes,)), sems((3 * planes,)),
            sems((CHUNKS,)), sems((CHUNKS,)), sems((hops,)), sems((hops,)),
            sems((hops,)), sems((hops,)), sems((planes + 1,)), sems((planes + 1,)),
        ],
        compiler_params=pltpu.CompilerParams(
            collective_id=0, has_side_effects=True, vmem_limit_bytes=60 << 20
        ),
    )(
        section_inputs.reshape(tokens, channels),
        mix_weight[0],
        out_cotangent.reshape(tokens, channels),
        norm_gain,
        positions,
    )
    weight_grad, gain_share, grads = pl.pallas_call(
        store_kernel,
        out_shape=tuple(jax.ShapeDtypeStruct(r.shape, r.dtype) for r in results),
        in_specs=[vmem] * 3,
        out_specs=(hbm,) * 3,
        scratch_shapes=[sems((3,))],
    )(*results)
    return (grads.reshape(1, micro, tok_mb, channels), weight_grad[None], gain_share)


def solution(mesh):
    return jax.shard_map(
        body,
        mesh=mesh,
        in_specs=(
            P("section", None, "dp", None),
            P("section", None, None),
            P("section", None),
            P(None, "dp", None),
            P(None, "dp"),
        ),
        out_specs=(P("section", None, "dp", None), P("section", "dp", None), P("section", "dp")),
        check_vma=False,
    )
```

time: 85.1 us -> 75.8 us (0.89)
  local copies, waits for them, and re-layouts: 4.38 us -> 0 us
  Pallas kernels: 79.1 us -> 75 us
    pallas_call x1, Pallas kernels: 79.1 us -> 72.1 us  [body(): pl.pallas_call(functools.partial(back_kernel, planes, sections), out_shap...]
    unnamed x6 -> x0, local copies, waits for them, and re-layouts: 3.86 us -> none
    pallas_call x0 -> x1, Pallas kernels: none -> 2.89 us  [body(): pl.pallas_call(store_kernel, out_shape=tuple((jax.ShapeDtypeStruct(r.shap...]
where the time goes in v1:
time: 75.8 us; the launch traced here: 75.7 us
  Pallas kernels  75 us (99%)
    pallas_call x1, Pallas kernels, body(): pl.pallas_call(functools.partial(back_kernel, planes, sections), out_shap...  72.1 us
    pallas_call x1, Pallas kernels, body(): pl.pallas_call(store_kernel, out_shape=tuple((jax.ShapeDtypeStruct(r.shap...  2.89 us

profile of v1, /device:TPU:0, one launch (start us, length us, event | category | flops | bytes accessed | tf_op | source)
XLA Modules:
  0.0 75.7 jit_solution(17465698168134942856)
XLA Ops:
  0.6 72.1 %shard_map.76 = (f32[128,2048]{1,0:T(8,128)}, f32[1,128]{1,0:T(1,128)}, bf16[256,2048]{1,0:T(8,128)(2,1)}) custom-call(bf16[256,2048]{1,0:T(8,128)(2,1)} %bitcast.6, bf16[2048,2048]{1,0:T(8,128)(2,1)} %bitcast.5, bf16[256,2048]{1,0:T(8,128)(2,1)} %bitcast.7, f32[1,2048]{1,0:T(1,128)} %gain_hbm.1, s32[2,128]{1,0:T(2,128)} %pos_hbm.1), custom_call_target="tpu_custom_call" | custom-call | tf_op jit(solution)/shard_map/pallas_call | solution.py:525
  72.8 2.9 %shard_map.77 = (f32[128,2048]{1,0:T(8,128)}, f32[1,128]{1,0:T(1,128)}, bf16[256,2048]{1,0:T(8,128)(2,1)}) custom-call(f32[128,2048]{1,0:T(8,128)} %get-tuple-element.9.refs_0_, f32[1,128]{1,0:T(1,128)} %get-tuple-element.10.refs_1_, bf16[256,2048]{1,0:T(8,128)(2,1)} %get-tuple-element.11.refs_2_), custom_call_target="tpu_custom_call" | custom-call | tf_op jit(solution)/shard_map/pallas_call | solution.py:577

commit v2 on v1

--- a/solution.py
+++ b/solution.py
@@ -15,6 +15,7 @@
 ROOT = math.sqrt(2.0 / math.pi)
 CUBE = 0.044715
 CHUNKS = 4
+GRANT = 52736
 
 
 def contract(a, b, dims):
@@ -23,8 +24,7 @@
 
 def block_order(planes, chunks):
     pairs = planes // 2
-    first = [(i, k) for i in range(pairs) for k in range(2)]
-    return first + [(i, k) for k in range(2, chunks) for i in range(pairs)]
+    return [(i, k + n) for k in range(0, chunks, 2) for i in range(pairs) for n in range(2)]
 
 
 def back_kernel(
@@ -150,18 +150,18 @@
 
     arrived = set()
 
-    def arrive(name, sent):
-        if name not in arrived:
+    def arrive(name, sent, again=False):
+        if again or name not in arrived:
             arrived.add(name)
             with jax.named_scope("w_" + name):
                 sent.wait_recv()
 
     def forward_u(k):
-        arrive("ux%d" % k, ux[k])
+        arrive("ux%d" % k, ux[k], True)
         ud[k].start()
 
     def forward_a(b):
-        arrive("ay%d" % b, ay[b])
+        arrive("ay%d" % b, ay[b], True)
         ad[b].start()
 
     def upstream(mb):
@@ -218,10 +218,11 @@
                 low = c * 128 % rows
                 n = x_ref[r, cols].astype(F32) * q * gain_ref[:, cols]
                 n2 = n * n
-                th = jnp.tanh(ROOT * (n + CUBE * (n2 * n)))
-                cdf = 0.5 * (1.0 + th)
+                th = jnp.tanh(n * (ROOT + (ROOT * CUBE) * n2))
+                cdf = 0.5 + 0.5 * th
                 tmp[c * 128 // rows, r, low:low + 128] = (n * cdf).astype(BF16)
-                slope[r, cols] = cdf + (0.5 * ROOT) * n * (1.0 - th * th) * (1.0 + (3.0 * CUBE) * n2)
+                bend = n * (0.5 * ROOT + (1.5 * ROOT * CUBE) * n2)
+                slope[r, cols] = cdf + bend * (1.0 - th * th)
 
         for side in range(2):
             act_ref[side, spans[b], :] = contract(eye_ref[...], tmp[side], ((1,), (1,))).astype(BF16)
@@ -249,7 +250,10 @@
             ay[b].start()
             ax[b].start()
 
-    forward_u(0)
+    @pl.when(sec == last)
+    def _():
+        forward_u(0)
+
     with jax.named_scope("w_w"):
         load_w.wait()
 
@@ -274,16 +278,27 @@
                 gain_own[:, piece] = jnp.sum(grad_norm * xc * q, axis=0, keepdims=True)
             proj[...] = lanes
 
+    def send_rest():
+        for b in order[2:]:
+            ay[b].start()
+            ax[b].start()
+
     steps = channels // width
     back_columns(0, steps // 4)
-    forward_a(order[0])
+
+    @pl.when(sec == last)
+    def _():
+        forward_a(order[0])
+
     back_columns(steps // 4, steps // 2)
-    forward_a(order[1])
-    ux[1].start()
-    for b in order[2:]:
-        ay[b].start()
-        ax[b].start()
-    uy[1].start()
+
+    @pl.when(sec == last)
+    def _():
+        forward_a(order[1])
+        ux[1].start()
+        send_rest()
+        uy[1].start()
+
     back_columns(steps // 2, steps)
     gain_x.start()
 
@@ -302,6 +317,15 @@
         @pl.when(sec > 0)
         def _():
             relay(mb).start()
+
+    @pl.when(sec < last)
+    def _():
+        forward_u(0)
+        ux[1].start()
+        uy[1].start()
+        for b in order[:2]:
+            forward_a(b)
+        send_rest()
 
     z_next = lax.rem(me + 4, total)
     z_prev = lax.rem(me + total - 4, total)
@@ -416,12 +440,12 @@
             reach[i, k] += 1
 
     begin(0, 0)
+    forward_u(1)
     for b in order[2:]:
         forward_a(b)
     for k in range(2, CHUNKS):
         ux[k].start()
         uy[k].start()
-    forward_u(1)
     advance(0, 0)
     begin(0, 1)
     advance(0, 0)
@@ -429,7 +453,8 @@
         begin(i, 0)
         begin(i, 1)
     advance(0, 1)
-    forward_u(2)
+    for k in range(2, CHUNKS):
+        forward_u(k)
     arrive("gain_x", gain_x)
     gain_mid[...] = gain_own[...] + gain_in[0]
     gain_y.start()
@@ -438,14 +463,15 @@
     advance(0, 1)
     for i in range(1, pairs):
         advance(i, 1)
-    for k in range(2, CHUNKS):
-        if k + 1 < CHUNKS:
-            forward_u(k + 1)
-        for i in range(pairs):
+    for k in range(2, CHUNKS, 2):
+        begin(0, k)
+        begin(0, k + 1)
+        advance(0, k)
+        for i in range(1, pairs):
             begin(i, k)
-        if k + 1 < CHUNKS:
-            for i in range(pairs):
-                advance(i, k)
+        advance(0, k + 1)
+        for i in range(1, pairs):
+            begin(i, k + 1)
         if k == 2:
             arrive("gain_y", gain_y)
             gain_sum[...] = gain_mid[...] + gain_in[1]
@@ -565,7 +591,7 @@
             sems((hops,)), sems((hops,)), sems((planes + 1,)), sems((planes + 1,)),
         ],
         compiler_params=pltpu.CompilerParams(
-            collective_id=0, has_side_effects=True, vmem_limit_bytes=60 << 20
+            collective_id=0, has_side_effects=True, vmem_limit_bytes=GRANT << 10
         ),
     )(
         section_inputs.reshape(tokens, channels),
@@ -580,6 +606,7 @@
         in_specs=[vmem] * 3,
         out_specs=(hbm,) * 3,
         scratch_shapes=[sems((3,))],
+        compiler_params=pltpu.CompilerParams(vmem_limit_bytes=4 << 20),
     )(*results)
     return (grads.reshape(1, micro, tok_mb, channels), weight_grad[None], gain_share)
 

time: 75.8 us -> 71.4 us (0.942)
  Pallas kernels: 75 us -> 69.1 us
  local copies, waits for them, and re-layouts: 0 us -> 1.37 us
    pallas_call x1, Pallas kernels: 72.1 us -> 67.8 us  [body(): pl.pallas_call(functools.partial(back_kernel, planes, sections), out_shap...]
    pallas_call x1, Pallas kernels: 2.89 us -> 1.35 us  [body(): pl.pallas_call(store_kernel, out_shape=tuple((jax.ShapeDtypeStruct(r.shap...]
    unnamed x0 -> x4, local copies, waits for them, and re-layouts: none -> 1.37 us
where the time goes in v2:
time: 71.4 us; the launch traced here: 71.2 us
  Pallas kernels  69.1 us (97%)
  local copies, waits for them, and re-layouts  1.37 us (2%)
    pallas_call x1, Pallas kernels, body(): pl.pallas_call(functools.partial(back_kernel, planes, sections), out_shap...  67.8 us

profile of v2, /device:TPU:0, one launch (start us, length us, event | category | flops | bytes accessed | tf_op | source)
XLA Modules:
  0.0 71.2 jit_solution(4597041350201352196)
XLA Ops:
  0.6 0.0 copy-start
  0.6 0.7 copy-done
  1.3 0.0 copy-start.1
  1.3 0.7 copy-done.1
  2.0 67.8 %shard_map.76 = (f32[128,2048]{1,0:T(8,128)S(1)}, f32[1,128]{1,0:T(1,128)S(1)}, bf16[256,2048]{1,0:T(8,128)(2,1)S(1)}) custom-call(bf16[256,2048]{1,0:T(8,128)(2,1)} %bitcast.6, bf16[2048,2048]{1,0:T(8,128)(2,1)} %bitcast.5, bf16[256,2048]{1,0:T(8,128)(2,1)} %bitcast.7, f32[1,2048]{1,0:T(1,128)S(1)} %copy-done, s32[2,128]{1,0:T(2,128)S(1)} %copy-done.1), custom_call_target="tpu_custom_call" | custom-call | tf_op jit(solution)/shard_map/pallas_call | solution.py:551
  69.8 1.3 %shard_map.77 = (f32[128,2048]{1,0:T(8,128)}, f32[1,128]{1,0:T(1,128)}, bf16[256,2048]{1,0:T(8,128)(2,1)}) custom-call(f32[128,2048]{1,0:T(8,128)S(1)} %get-tuple-element.9.refs_0_, f32[1,128]{1,0:T(1,128)S(1)} %get-tuple-element.10.refs_1_, bf16[256,2048]{1,0:T(8,128)(2,1)S(1)} %get-tuple-element.11.refs_2_), custom_call_target="tpu_custom_call" | custom-call | tf_op jit(solution)/shard_map/pallas_call | solution.py:603
Async XLA Ops:
  0.6 0.7 copy-start
  1.3 0.7 copy-start.1

commit v3 on v2

--- a/solution.py
+++ b/solution.py
@@ -244,15 +244,12 @@
             with jax.named_scope("w_relay%d" % mb):
                 relay(mb).wait_recv()
             upstream(mb)
-        ux[0].start()
-        uy[0].start()
-        for b in order[:2]:
-            ay[b].start()
-            ax[b].start()
 
     @pl.when(sec == last)
     def _():
         forward_u(0)
+        ux[1].start()
+        uy[1].start()
 
     with jax.named_scope("w_w"):
         load_w.wait()
@@ -295,12 +292,22 @@
     @pl.when(sec == last)
     def _():
         forward_a(order[1])
-        ux[1].start()
         send_rest()
-        uy[1].start()
+
+    @pl.when(sec < last)
+    def _():
+        ux[0].start()
+        uy[0].start()
+        for b in order[:2]:
+            ay[b].start()
+            ax[b].start()
 
     back_columns(steps // 2, steps)
     gain_x.start()
+
+    @pl.when(sec == last)
+    def _():
+        forward_u(1)
 
     for mb in range(micro):
         @pl.loop(mb * (tok_mb // step_rows), (mb + 1) * (tok_mb // step_rows))
@@ -326,6 +333,9 @@
         for b in order[:2]:
             forward_a(b)
         send_rest()
+        forward_u(1)
+        for b in order[2:]:
+            forward_a(b)
 
     z_next = lax.rem(me + 4, total)
     z_prev = lax.rem(me + total - 4, total)
@@ -440,9 +450,12 @@
             reach[i, k] += 1
 
     begin(0, 0)
-    forward_u(1)
-    for b in order[2:]:
-        forward_a(b)
+
+    @pl.when(sec == last)
+    def _():
+        for b in order[2:]:
+            forward_a(b)
+
     for k in range(2, CHUNKS):
         ux[k].start()
         uy[k].start()
@@ -488,7 +501,21 @@
             done += 1
     for k in range(done, CHUNKS):
         finish(k)
-        settle(k - 1)
+        if k < CHUNKS - 1:
+            settle(k - 1)
+    for sent in [gain_x, gain_y] + ux + uy + ud + ax + ay + ad + gain_zs:
+        sent.wait_send()
+    for k in range(CHUNKS):
+        for d in range(planes):
+            @pl.when(d > z)
+            def _():
+                right(k * planes + d).wait_send()
+
+            @pl.when(d < z)
+            def _():
+                left(k * planes + d).wait_send()
+
+    settle(CHUNKS - 2)
     with jax.named_scope("w_gain"):
         for tiny in gain_zs:
             tiny.wait_recv()
@@ -502,17 +529,8 @@
             gain_out[...] = gain_z[0, :, r * (channels // total):(r + 1) * (channels // total)]
     settle(CHUNKS - 1)
 
-    for sent in [gain_x, gain_y] + ux + uy + ud + ax + ay + ad + swaps + gain_zs:
+    for sent in swaps:
         sent.wait_send()
-    for k in range(CHUNKS):
-        for d in range(planes):
-            @pl.when(d > z)
-            def _():
-                right(k * planes + d).wait_send()
-
-            @pl.when(d < z)
-            def _():
-                left(k * planes + d).wait_send()
 
     @pl.when(sec > 0)
     def _():

time: 71.4 us -> 70.2 us (0.983)
  Pallas kernels: 69.1 us -> 68 us
    pallas_call x1, Pallas kernels: 67.8 us -> 66.6 us  [body(): pl.pallas_call(functools.partial(back_kernel, planes, sections), out_shap...]
where the time goes in v3:
time: 70.2 us; the launch traced here: 70 us
  Pallas kernels  68 us (97%)
  local copies, waits for them, and re-layouts  1.37 us (2%)
    pallas_call x1, Pallas kernels, body(): pl.pallas_call(functools.partial(back_kernel, planes, sections), out_shap...  66.6 us

profile of v3, /device:TPU:0, one launch (start us, length us, event | category | flops | bytes accessed | tf_op | source)
XLA Modules:
  0.0 70.0 jit_solution(3601243052155504390)
XLA Ops:
  0.6 0.0 copy-start
  0.6 0.7 copy-done
  1.3 0.0 copy-start.1
  1.3 0.7 copy-done.1
  2.0 66.6 %shard_map.76 = (f32[128,2048]{1,0:T(8,128)S(1)}, f32[1,128]{1,0:T(1,128)S(1)}, bf16[256,2048]{1,0:T(8,128)(2,1)S(1)}) custom-call(bf16[256,2048]{1,0:T(8,128)(2,1)} %bitcast.6, bf16[2048,2048]{1,0:T(8,128)(2,1)} %bitcast.5, bf16[256,2048]{1,0:T(8,128)(2,1)} %bitcast.7, f32[1,2048]{1,0:T(1,128)S(1)} %copy-done, s32[2,128]{1,0:T(2,128)S(1)} %copy-done.1), custom_call_target="tpu_custom_call" | custom-call | tf_op jit(solution)/shard_map/pallas_call | solution.py:569
  68.6 1.3 %shard_map.77 = (f32[128,2048]{1,0:T(8,128)}, f32[1,128]{1,0:T(1,128)}, bf16[256,2048]{1,0:T(8,128)(2,1)}) custom-call(f32[128,2048]{1,0:T(8,128)S(1)} %get-tuple-element.9.refs_0_, f32[1,128]{1,0:T(1,128)S(1)} %get-tuple-element.10.refs_1_, bf16[256,2048]{1,0:T(8,128)(2,1)S(1)} %get-tuple-element.11.refs_2_), custom_call_target="tpu_custom_call" | custom-call | tf_op jit(solution)/shard_map/pallas_call | solution.py:621
Async XLA Ops:
  0.6 0.7 copy-start
  1.3 0.7 copy-start.1
